TPU v7x, 32 devices: a whole 2x2x4 slice. The times are simulated.
32 devices in a mesh: wall: 8 (over y, x, core), vec: 4 (over z).
Axes of the slice: x: 2, y: 2, z: 4, core: 2. Of those that a mesh axis runs over, the one named last changes fastest.
Arguments:
- perturbation: float32 [8, 3, 96, 8, 384], P('vec', None, 'wall'), may hold values from -6 to 6
- prev_term: bfloat16 [8, 3, 96, 8, 384], P('vec', None, 'wall'), may hold values from -6 to 6
- base_store: bfloat16 [8, 3, 96, 8, 384], P('vec', None, 'wall'), may hold values from -4 to 4
- step_index: int32 [1], replicated, may hold values from 0 to 32767
- slot_of_step: int32 [8], replicated, may hold values from 0 to 7, each once
- span_shift: int32 [1], replicated, may hold values from 0 to 383
- lower_gap: float32 [96], P('wall'), may hold values from 0.0005 to 0.012
- pivots: float32 [96], P('wall'), may hold values from 300 to 303
- upper_coef: float32 [96], P('wall'), may hold values from 297 to 300
Outputs:
- advanced: float32 [8, 3, 96, 8, 384], P('vec', None, 'wall')
- advection: bfloat16 [8, 3, 96, 8, 384], P('vec', None, 'wall')
Inputs may be any that keep to these rules, and one draw needn't show every extreme that they name: `slot_of_step`: slot s lies at position s % 2 of the steps held by index s // 2 of vec.
All inputs are finite; a program needn't handle non-finite values.
Results may differ from a plain program's by a relative error of at most 0.0025.
Values may be sent and summed in bfloat16 or wider, within the bound.
A program may use at most 64 MiB of HBM per device.

v0:
```python
import jax
import jax.numpy as jnp
from jax import lax
from jax.sharding import PartitionSpec as P

STEP_SIZE = 0.5
NEW_WEIGHT = 5.0 / 12.0
OLD_WEIGHT = -17.0 / 60.0
VISCOUS_WEIGHT = -0.06


def broadcast(value, axis, source):
    kept = jnp.where(lax.axis_index(axis) == source, value, 0).astype(value.dtype)
    return lax.psum(kept, axis)


def padded_2(cells, sides, width):
    for axis, dim in sides:
        count = lax.axis_size(axis)
        ends = count - 1
        head = lax.slice_in_dim(cells, 0, width, axis=dim)
        tail = lax.slice_in_dim(cells, cells.shape[dim] - width, cells.shape[dim], axis=dim)
        cells = jnp.concatenate(
            [
                lax.ppermute(tail, axis, [(i, (i + 1) % count) for i in range(ends)]),
                cells,
                lax.ppermute(head, axis, [((i + 1) % count, i) for i in range(ends)]),
            ],
            axis=dim,
        )
    return cells


def periodic_diff(field, along):
    return 0.5 * (jnp.roll(field, -1, along) - jnp.roll(field, 1, along))


def lower_matrix(decays):
    count = decays.shape[0]
    row_out = jnp.arange(count)[:, None, None]
    row_in = jnp.arange(count)[None, :, None]
    row_mid = jnp.arange(count)[None, None, :]
    inside = (row_mid > row_in) & (row_mid <= row_out)
    products = jnp.prod(jnp.where(inside, decays[None, None, :], 1.0), axis=2)
    keep_mask = jnp.arange(count)[None, :] <= jnp.arange(count)[:, None]
    return jnp.where(keep_mask, products, 0.0)


def upper_matrix(ratios, pivots):
    count = ratios.shape[0]
    row_out = jnp.arange(count)[:, None, None]
    row_in = jnp.arange(count)[None, :, None]
    row_mid = jnp.arange(count)[None, None, :]
    inside = (row_mid >= row_out) & (row_mid < row_in)
    products = jnp.prod(jnp.where(inside, ratios[None, None, :], 1.0), axis=2)
    keep_mask = jnp.arange(count)[None, :] >= jnp.arange(count)[:, None]
    return jnp.where(keep_mask, products / pivots[None, :], 0.0)


def apply_rows(matrix, values):
    return jnp.einsum("ji,vcixz->vcjxz", matrix, values, precision=lax.Precision.HIGHEST)


def fold_with(weights, running, pieces):
    return running + jnp.einsum("r,rvcxz->vcxz", weights, pieces, precision=lax.Precision.HIGHEST)


def on_device(
    perturbation,
    prev_term,
    base_store,
    step_index,
    slot_of_step,
    span_shift,
    lower_gap,
    pivots,
    upper_coef,
):
    stored = base_store.shape[0]
    span_cells = perturbation.shape[4]
    slab_rows = perturbation.shape[2]
    step_count = slot_of_step.shape[0]
    orbit_step = step_index[0] % step_count
    slot_index = slot_of_step[orbit_step]
    owner_index = slot_index // stored
    local_slab = lax.dynamic_index_in_dim(base_store, slot_index % stored, 0, keepdims=False)
    base_slab = broadcast(local_slab, "vec", owner_index)
    doubled = jnp.concatenate([base_slab, base_slab], axis=3)
    offset = (span_cells - span_shift[0]) % span_cells
    base_field = lax.dynamic_slice_in_dim(doubled, offset, span_cells, 3).astype(jnp.float32)
    padded = padded_2(perturbation, (("wall", 2),), 1)
    above = padded[:, :, 2:]
    below = padded[:, :, :-2]
    explicit = -(
        base_field[0] * periodic_diff(perturbation, 3)
        + base_field[1] * (0.5 * (above - below))
        + base_field[2] * periodic_diff(perturbation, 4)
    )
    advection = explicit.astype(jnp.bfloat16)
    source = (
        perturbation
        + STEP_SIZE * (NEW_WEIGHT * explicit + OLD_WEIGHT * prev_term.astype(jnp.float32))
        + VISCOUS_WEIGHT * (above - 2.0 * perturbation + below)
    )
    decays = 1.0 - lower_gap
    ratios = upper_coef / pivots
    into_rows = jnp.cumprod(decays)
    from_top = jnp.cumprod(ratios[::-1])[::-1]
    swept_local = apply_rows(lower_matrix(decays), source)
    forward_value = swept_local[:, :, slab_rows - 1]
    all_gap, all_pivots, all_upper = (
        lax.all_gather(lower_gap, "wall", axis=0, tiled=True),
        lax.all_gather(pivots, "wall", axis=0, tiled=True),
        lax.all_gather(upper_coef, "wall", axis=0, tiled=True),
    )
    wall_count = lax.axis_size("wall")
    own_index = lax.axis_index("wall")
    forward_coef = jnp.prod((1.0 - all_gap).reshape(wall_count, slab_rows), axis=1)
    backward_coef = jnp.prod((all_upper / all_pivots).reshape(wall_count, slab_rows), axis=1)
    device_ids = jnp.arange(wall_count)
    source_dev = device_ids[:, None]
    middle_dev = device_ids[None, :]
    forward_weights = jnp.where(
        device_ids < own_index,
        jnp.prod(
            jnp.where(
                (middle_dev > source_dev) & (middle_dev < own_index), forward_coef[None, :], 1.0
            ),
            axis=1,
        ),
        0.0,
    )
    backward_weights = jnp.where(
        device_ids > own_index,
        jnp.prod(
            jnp.where(
                (middle_dev < source_dev) & (middle_dev > own_index), backward_coef[None, :], 1.0
            ),
            axis=1,
        ),
        0.0,
    )
    forward_in = fold_with(
        forward_weights,
        jnp.zeros_like(forward_value),
        lax.all_gather(forward_value[None], "wall", axis=0, tiled=True),
    )
    swept = swept_local + into_rows[None, None, :, None, None] * forward_in[:, :, None]
    solved_local = apply_rows(upper_matrix(ratios, pivots), swept)
    backward_value = solved_local[:, :, 0]
    backward_in = fold_with(
        backward_weights,
        jnp.zeros_like(backward_value),
        lax.all_gather(
            backward_value[None].astype(jnp.bfloat16), "wall", axis=0, tiled=True
        ).astype(jnp.float32),
    )
    advanced = solved_local + from_top[None, None, :, None, None] * backward_in[:, :, None]
    return (advanced, advection)


def solution(mesh):
    return jax.shard_map(
        on_device,
        mesh=mesh,
        in_specs=(
            P("vec", None, "wall", None, None),
            P("vec", None, "wall", None, None),
            P("vec", None, "wall", None, None),
            P(),
            P(),
            P(),
            P("wall"),
            P("wall"),
            P("wall"),
        ),
        out_specs=(P("vec", None, "wall", None, None), P("vec", None, "wall", None, None)),
        check_vma=False,
    )
```

profile of v0, /device:TPU:0, one launch (start us, length us, event | category | flops | bytes accessed | tf_op | source)
XLA Modules:
  0.0 99.0 jit_solution(1753203695972538550)
XLA Ops:
  7.2 0.0 copy-start
  7.2 0.0 all-reduce.6.cloned.1.call-start
  8.0 1.2 %dynamic_slice.10 = s32[1]{0:T(128)} dynamic-slice(s32[8]{0:T(128)} %param.13, s32[]{:T(128)S(6)} %select_n.69), dynamic_slice_sizes={1} | dynamic-slice | bytes 12 | tf_op jit(solution)/shard_map/dynamic_slice | solution.py:84
  11.8 1.7 %select_bitcast_fusion = bf16[3,12,8,384]{3,2,1,0:T(8,128)(2,1)} fusion(bf16[2,3,12,8,384]{4,3,2,1,0:T(8,128)(2,1)} %param.11, s32[]{:T(128)S(6)} %select_n.73, pred[]{:T(512)S(6)} %eq.7), kind=kLoop, calls=%fused_computation.26 | loop fusion | flops 110592 | bytes 442373 | tf_op jit(solution)/shard_map/jit(_where)/select_n | solution.py:13
  13.5 0.0 all-reduce.6.cloned.1.call-update
  13.5 1.6 %fusion.44 = (f32[2,3,1,8,384]{4,3,2,1,0:T(8,128)}, f32[2,3,1,8,384]{4,3,2,1,0:T(8,128)}) fusion(f32[2,3,12,8,384]{4,3,2,1,0:T(8,128)} %param.9), kind=kLoop, calls=%fused_computation.74 | loop fusion | bytes 294912 | tf_op jit(solution)/shard_map/slice | solution.py:21
  15.1 1.3 %collective-permute-start = (f32[2,3,1,8,384]{4,3,2,1,0:T(8,128)}, f32[2,3,1,8,384]{4,3,2,1,0:T(8,128)}, u32[]{:S(2)}, u32[]{:S(2)}) collective-permute-start(f32[2,3,1,8,384]{4,3,2,1,0:T(8,128)} %get-tuple-element.19), channel_id=1, source_target_pairs={{4,0},{8,4},{12,8},{16,12},{20,16},{24,20},{28,24},{5,1},{9,5},{13... | collective-permute-start | bytes 221192 | tf_op jit(solution)/shard_map/ppermute | solution.py:27
  16.4 3.7 %collective-permute-start.1 = (f32[2,3,1,8,384]{4,3,2,1,0:T(8,128)}, f32[2,3,1,8,384]{4,3,2,1,0:T(8,128)}, u32[]{:S(2)}, u32[]{:S(2)}) collective-permute-start(f32[2,3,1,8,384]{4,3,2,1,0:T(8,128)} %get-tuple-element.20), channel_id=1, source_target_pairs={{0,4},{4,8},{8,12},{12,16},{16,20},{20,24},{24,28},{1,5},{5,9},{9,... | collective-permute-start | bytes 221192 | tf_op jit(solution)/shard_map/ppermute | solution.py:25
  20.7 0.1 fusion.42
  20.9 0.0 copy-start.12
  20.9 0.0 copy-start.5
  20.9 1.2 %fusion.45 = (f32[2,3,12,8,383]{4,3,2,1,0:T(8,128)S(1)}, f32[2,3,12,8,383]{4,3,2,1,0:T(8,128)}) fusion(f32[2,3,12,8,384]{4,3,2,1,0:T(8,128)S(1)} %copy-done), kind=kLoop, calls=%fused_computation.75 | loop fusion | bytes 3529728 | tf_op jit(solution)/shard_map/jit(_roll_static)/slice | solution.py:35
  22.1 0.8 fusion.43
  22.9 0.6 iota_compare_fusion.2
  23.5 0.6 iota_compare_fusion.9
  24.1 0.5 iota_compare_fusion.8
  24.6 0.5 fusion.39
  25.1 1.3 %dynamic-slice = u32[1]{0:T(128)} dynamic-slice(u32[32]{0:T(128)} %constant.90, u32[]{:T(128)S(6)} %add.61), dynamic_slice_sizes={1} | dynamic-slice | bytes 12
  27.2 0.6 broadcast.73.clone
  27.7 1.3 %dynamic-update-slice = f32[96]{0:T(128)} dynamic-update-slice(f32[96]{0:T(128)} %broadcast.73.clone, f32[12]{0:T(128)S(1)} %copy-done.12, u32[]{:T(128)} %bitcast.12) | dynamic-update-slice | bytes 100
  29.1 0.6 broadcast.73.clone.1
  29.6 1.3 %dynamic-update-slice.1 = f32[96]{0:T(128)} dynamic-update-slice(f32[96]{0:T(128)} %broadcast.73.clone.1, f32[12]{0:T(128)} %param.17, u32[]{:T(128)} %bitcast.12) | dynamic-update-slice | bytes 100
  30.9 0.0 copy-done.5
  31.0 0.7 div.25
  31.6 0.5 broadcast.73.clone.2
  32.1 1.2 %dynamic-update-slice.2 = f32[96]{0:T(128)} dynamic-update-slice(f32[96]{0:T(128)} %broadcast.73.clone.2, f32[12]{0:T(128)S(1)} %copy-done.5, u32[]{:T(128)} %bitcast.12) | dynamic-update-slice | bytes 100
  33.3 15.7 %all-reduce.3 = (f32[96]{0:T(128)S(1)}, f32[96]{0:T(128)}, f32[96]{0:T(128)}) all-reduce(f32[96]{0:T(128)} %dynamic-update-slice, f32[96]{0:T(128)} %dynamic-update-slice.1, f32[96]{0:T(128)} %dynamic-update-slice.2), channel_id=1, replica_groups=mesh['wall'=8,'vec'=4] {'wall'}, use_global_device_ids=true, to_apply=%add | all-reduce | flops 288 | bytes 2304
  49.0 0.5 broadcast_subtract_fusion
  49.5 0.7 reshape.167
  50.2 0.6 reduce_prod.55
  50.8 1.3 %reduce-window.17 = f32[12,1]{0,1:T(1,128)} reduce-window(f32[12,1]{0,1:T(1,128)} %get-tuple-element.28, f32[]{:T(128)} %constant.78.clone.1), window={size=12x1 pad=11_0x0_0}, to_apply=%region_2.3 | reduce-window | flops 132 | bytes 100 | tf_op jit(solution)/shard_map/reduce-window.7
  52.2 1.2 %div.28 = f32[96]{0:T(128)} divide(f32[96]{0:T(128)} %get-tuple-element.11, f32[96]{0:T(128)} %get-tuple-element.12) | non-fusion elementwise | flops 96 | bytes 1152 | tf_op jit(solution)/shard_map/div | solution.py:119
  53.4 0.7 reshape.170
  54.1 0.6 reduce_prod.58
  54.7 0.7 rev.6
  55.4 0.9 reduce-window.18
  56.2 0.6 rev.7
  56.8 1.4 %select_reduce_fusion.3 = f32[8]{0:T(128)} fusion(f32[8]{0:T(128)} %reduce_prod.55, pred[8]{0:T(512)(128)(4,1)} %iota_compare_fusion.9), kind=kLoop, calls=%fused_computation.50 | loop fusion | flops 248 | bytes 72 | tf_op jit(solution)/shard_map/reduce_prod | solution.py:125
  58.2 0.0 copy-done.9
  58.2 0.9 select_reduce_fusion
  59.1 1.3 %select_reduce_fusion.2 = f32[8]{0:T(128)} fusion(f32[8]{0:T(128)} %reduce_prod.58, pred[8]{0:T(512)(128)(4,1)} %iota_compare_fusion.8), kind=kLoop, calls=%fused_computation.47 | loop fusion | flops 248 | bytes 72 | tf_op jit(solution)/shard_map/reduce_prod | solution.py:135
  60.4 1.0 select_reduce_fusion.1
  61.4 0.9 fusion.46
  62.3 1.3 %fusion.15 = f32[3,12,8,384]{3,2,1,0:T(8,128)S(1)} fusion(s32[]{:T(128)S(6)} %select_n.77, bf16[3,12,8,384]{3,2,1,0:T(8,128)(2,1)} %all-reduce.6.cloned.1.call-done), kind=kLoop, calls=%fused_computation.25 | loop fusion | flops 442368 | bytes 663556 | tf_op jit(solution)/shard_map/convert_element_type | solution.py:90
  63.6 0.0 collective-permute-done
  63.6 0.0 collective-permute-done.1
  63.7 0.1 copy-done.3
  63.7 2.5 %fusion.40 = (bf16[2,3,12,8,384]{4,3,2,1,0:T(8,128)(2,1)}, f32[2,3,12,8,384]{4,3,2,1,0:T(8,128)S(1)}) fusion(f32[12,8,384]{2,1,0:T(8,128)S(1)} %get-tuple-element.26, f32[2,3,12,8,383]{4,3,2,1,0:T(8,128)S(1)} %copy-done.1, f32[2,3,12,8,1]{4,3,2,1,0:T(8,128)S(1)} %copy-done.3, f32[2,3,12,8,1]{4,3,2,1,0:T(8,128)S(1)} %copy-done.2, ...), kind=kLoop, calls=%fused_computation.71 | loop fusion | flops 3538944 | bytes 6340608 | tf_op jit(solution)/shard_map/convert_element_type | solution.py:99
  66.2 1.2 %multiply_add_fusion.1 = f32[2,3,12,8,384]{4,3,2,1,0:T(8,128)S(1)} fusion(f32[2,3,12,8,384]{4,3,2,1,0:T(8,128)S(1)} %copy-done, bf16[2,3,12,8,384]{4,3,2,1,0:T(8,128)(2,1)S(1)} %copy-done.4, f32[2,3,12,8,384]{4,3,2,1,0:T(8,128)S(1)} %get-tuple-element.14, f32[2,3,1,8,384]{4,3,2,1,0:T(8,128)} %collective-permute-done, ...), kind=kLoop, calls=%fused_computation.15 | loop fusion | flops 2875392 | bytes 3244032 | tf_op jit(solution)/shard_map/add | solution.py:101
  67.5 1.2 %convolution_bitcast_fusion.1 = f32[2,3,12,8,384]{4,2,3,1,0:T(8,128)S(1)} fusion(f32[2,3,12,8,384]{4,3,2,1,0:T(8,128)S(1)} %multiply_add_fusion.1, f32[12,12]{1,0:T(8,128)S(1)} %select_reduce_fusion.1), kind=kOutput, calls=%fused_computation.1 | convolution fusion | flops 31850784 | bytes 1770048 | tf_op jit(solution)/shard_map/ji,vcixz->vcjxz/dot_general | solution.py:61
  68.7 0.0 copy-start.6
  68.8 0.1 slice.82
  68.9 11.0 %all-gather = f32[16,3,1,8,384]{4,3,2,1,0:T(8,128)S(1)} all-gather(f32[2,3,1,8,384]{4,3,2,1,0:T(8,128)S(1)} %copy.20), channel_id=2, replica_groups=mesh['wall'=8,'vec'=4] {'wall'}, dimensions={0}, use_global_device_ids=true | all-gather | bytes 663552 | tf_op jit(solution)/shard_map/all_gather | solution.py:146
  79.8 0.0 copy-done.10
  79.8 0.7 fusion.8
  80.6 0.0 copy-done.6
  80.6 0.0 copy-done.7
  80.6 0.0 copy-start.8
  80.6 0.0 copy-start.11
  80.6 1.4 %convolution_bitcast_fusion = f32[2,3,12,8,384]{4,2,3,1,0:T(8,128)S(1)} fusion(f32[2,3,12,8,384]{4,2,3,1,0:T(8,128)S(1)} %convolution_bitcast_fusion.1, f32[2,3,8,384]{3,2,1,0:T(8,128)S(1)} %bitcast.54, f32[12]{0:T(128)S(1)} %bitcast.56, f32[12,12]{1,0:T(8,128)S(1)} %select_reduce_fusion, f32[12]{0:T(128)S(1)} %copy-done.6), kind=kOutput, calls=%fused_computation | convolution fusion | flops 32293296 | bytes 1843872 | tf_op jit(solution)/shard_map/ji,vcixz->vcjxz/dot_general | solution.py:61
  82.0 8.3 %all-gather.1 = bf16[16,3,1,8,384]{4,3,2,1,0:T(8,128)(2,1)S(1)} all-gather(bf16[2,3,1,8,384]{4,3,2,1,0:T(8,128)(2,1)S(1)} %copy.21), channel_id=3, replica_groups=mesh['wall'=8,'vec'=4] {'wall'}, dimensions={0}, use_global_device_ids=true | all-gather | bytes 331776 | tf_op jit(solution)/shard_map/all_gather | solution.py:154
  90.3 0.4 fusion.12
  90.7 0.2 multiply_add_fusion
  90.9 1.2 %copy.22 = f32[2,3,12,8,384]{4,3,2,1,0:T(8,128)} copy(f32[2,3,12,8,384]{4,2,3,1,0:T(8,128)S(1)} %multiply_add_fusion) | data formatting | bytes 1769472
  (22 shorter events, 0.1 us)
Async XLA Ops:
  7.2 13.5 %copy-start = (f32[2,3,12,8,384]{4,3,2,1,0:T(8,128)S(1)}, f32[2,3,12,8,384]{4,3,2,1,0:T(8,128)}, u32[]{:S(2)}) copy-start(f32[2,3,12,8,384]{4,3,2,1,0:T(8,128)} %param.9) | copy-start | bytes 2654212
  7.2 55.1 %all-reduce.6.cloned.1.call-start = ((), (), s32[]{:S(2)}) async-start(), calls=%async_computation | async-start | bytes 442368 | tf_op jit(solution)/shard_map/psum | solution.py:14
  15.1 48.5 %collective-permute-start = (f32[2,3,1,8,384]{4,3,2,1,0:T(8,128)}, f32[2,3,1,8,384]{4,3,2,1,0:T(8,128)}, u32[]{:S(2)}, u32[]{:S(2)}) collective-permute-start(f32[2,3,1,8,384]{4,3,2,1,0:T(8,128)} %get-tuple-element.19), channel_id=1, source_target_pairs={{4,0},{8,4},{12,8},{16,12},{20,16},{24,20},{28,24},{5,1},{9,5},{13... | collective-permute-start | bytes 221192 | tf_op jit(solution)/shard_map/ppermute | solution.py:27
  16.4 47.3 %collective-permute-start.1 = (f32[2,3,1,8,384]{4,3,2,1,0:T(8,128)}, f32[2,3,1,8,384]{4,3,2,1,0:T(8,128)}, u32[]{:S(2)}, u32[]{:S(2)}) collective-permute-start(f32[2,3,1,8,384]{4,3,2,1,0:T(8,128)} %get-tuple-element.20), channel_id=1, source_target_pairs={{0,4},{4,8},{8,12},{12,16},{16,20},{20,24},{24,28},{1,5},{5,9},{9,... | collective-permute-start | bytes 221192 | tf_op jit(solution)/shard_map/ppermute | solution.py:25
  20.9 3.8 %copy-start.12 = (f32[12]{0:T(128)S(1)}, f32[12]{0:T(128)}, u32[]{:S(2)}) copy-start(f32[12]{0:T(128)} %param.15) | copy-start | bytes 148
  20.9 10.1 %copy-start.5 = (f32[12]{0:T(128)S(1)}, f32[12]{0:T(128)}, u32[]{:S(2)}) copy-start(f32[12]{0:T(128)} %param.16) | copy-start | bytes 148
  31.6 26.6 %copy-start.9 = (f32[12]{0:T(128)}, f32[12]{0:T(128)S(1)}, u32[]{:S(2)}) copy-start(f32[12]{0:T(128)S(1)} %div.25) | copy-start | bytes 148
  62.3 1.4 %copy-start.1 = (f32[2,3,12,8,383]{4,3,2,1,0:T(8,128)S(1)}, f32[2,3,12,8,383]{4,3,2,1,0:T(8,128)}, u32[]{:S(2)}) copy-start(f32[2,3,12,8,383]{4,3,2,1,0:T(8,128)} %get-tuple-element.22) | copy-start | bytes 2647300
  62.3 1.4 %copy-start.2 = (f32[2,3,12,8,1]{4,3,2,1,0:T(8,128)S(1)}, f32[2,3,12,8,1]{4,3,2,1,0:T(8,128)}, u32[]{:S(2)}) copy-start(f32[2,3,12,8,1]{4,3,2,1,0:T(8,128)} %get-tuple-element.23) | copy-start | bytes 6916
  62.3 1.5 %copy-start.3 = (f32[2,3,12,8,1]{4,3,2,1,0:T(8,128)S(1)}, f32[2,3,12,8,1]{4,3,2,1,0:T(8,128)}, u32[]{:S(2)}) copy-start(f32[2,3,12,8,1]{4,3,2,1,0:T(8,128)} %get-tuple-element.24) | copy-start | bytes 6916
  63.7 2.5 %copy-start.4 = (bf16[2,3,12,8,384]{4,3,2,1,0:T(8,128)(2,1)S(1)}, bf16[2,3,12,8,384]{4,3,2,1,0:T(8,128)(2,1)}, u32[]{:S(2)}) copy-start(bf16[2,3,12,8,384]{4,3,2,1,0:T(8,128)(2,1)} %param.10) | copy-start | bytes 1327108
  67.5 12.3 %copy-start.10 = (f32[8]{0:T(128)S(1)}, f32[8]{0:T(128)}, u32[]{:S(2)}) copy-start(f32[8]{0:T(128)} %select_reduce_fusion.3) | copy-start | bytes 100
  68.7 11.8 %copy-start.6 = (f32[12]{0:T(128)S(1)}, f32[12]{0:T(128)}, u32[]{:S(2)}) copy-start(f32[12]{0:T(128)} %param.16) | copy-start | bytes 148
  68.8 11.8 %copy-start.7 = (f32[12,1]{0,1:T(1,128)S(1)}, f32[12,1]{0,1:T(1,128)}, u32[]{:S(2)}) copy-start(f32[12,1]{0,1:T(1,128)} %reduce-window.17) | copy-start | bytes 148
  80.6 9.7 %copy-start.8 = (f32[8]{0:T(128)S(1)}, f32[8]{0:T(128)}, u32[]{:S(2)}) copy-start(f32[8]{0:T(128)} %select_reduce_fusion.2) | copy-start | bytes 100
  80.6 10.1 %copy-start.11 = (f32[12]{0:T(128)S(1)}, f32[12]{0:T(128)}, u32[]{:S(2)}) copy-start(f32[12]{0:T(128)} %rev.7) | copy-start | bytes 148
Sparse Core Ops, SparseCore 0:
  13.6 37.6 all-reduce.5
where the time goes:
time: 99.6 us; the launch traced here: 99 us
  blocking collectives  34.9 us (35%)
  other arithmetic  19.5 us (20%)
  between operations  19 us (19%)
  local copies, waits for them, and re-layouts  16.7 us (17%)
  starting transfers between devices  4.99 us (5%)
  matrix products  3.7 us (4%)
    unnamed x1, blocking collectives  15.7 us
    all_gather x1, blocking collectives, on_device(): lax.all_gather(forward_value[None], 'wall', axis=0, tiled=True)  11 us
    all_gather x1, blocking collectives, on_device(): lax.all_gather(backward_value[None].astype(jnp.bfloat16), 'wall', axis=0,...  8.26 us
    unnamed x34, local copies, waits for them, and re-layouts  8.1 us
    ppermute x1, starting transfers between devices, padded_2(): lax.ppermute(tail, axis, [(i, (i + 1) % count) for i in range(ends)])  3.67 us
    slice x4, local copies, waits for them, and re-layouts, periodic_diff(): return 0.5 * (jnp.roll(field, -1, along) - jnp.roll(field, 1, along))  3.02 us
    another operation x3, other arithmetic  2.71 us
    dot_general x2, matrix products, apply_rows(): jnp.einsum('ji,vcixz->vcjxz', matrix, values, precision=lax.Precision.HIG...  2.59 us
  transfers between devices with their start and end apart: 3, of which 0 were waited for; matrix products, arithmetic and copies ran while one was open for 28% of the time, Pallas kernels for 0%

commit v1 on v0

v1 whole, which is shorter than its diff:
```python
import functools

import jax
import jax.numpy as jnp
from jax import lax
from jax.experimental import pallas as pl
from jax.experimental.pallas import tpu as pltpu
from jax.sharding import PartitionSpec as P

STEP_SIZE = 0.5
NEW_WEIGHT = 5.0 / 12.0
OLD_WEIGHT = -17.0 / 60.0
VISCOUS_WEIGHT = -0.06
CHUNK_ROWS = 2
HOP_LAG = 2


def kernel(
    W,
    V,
    q_hbm,
    prev_hbm,
    bs_hbm,
    step_s,
    slots_s,
    shift_s,
    gap_s,
    piv_s,
    up_s,
    adv_hbm,
    advec_hbm,
    qpad,
    prev_v,
    bs_v,
    from_l,
    from_r,
    out_r,
    out_l,
    loc,
    expl,
    adv_v,
    fcar,
    bcar,
    fsend,
    esend,
    cin,
    ctile,
    ctiles,
    tab_d,
    tab_w,
    tab_p,
    tab_rho,
    tab_a,
    tab_c,
    in_sem,
    halo_send,
    halo_recv,
    coef_send,
    coef_recv,
    lr_send,
    lr_recv,
    rl_send,
    rl_recv,
    car_send,
    car_recv,
    out_sem,
):
    w = lax.axis_index("wall")
    v = lax.axis_index("vec")
    nvec, ncomp, rows, nx, nz = q_hbm.shape
    stored = bs_hbm.shape[0]
    fields = nvec * ncomp
    chunks = rows // CHUNK_ROWS

    q_in = pltpu.make_async_copy(q_hbm, qpad.at[:, :, pl.ds(1, rows)], in_sem.at[0])
    prev_in = pltpu.make_async_copy(prev_hbm, prev_v, in_sem.at[1])
    bs_in = pltpu.make_async_copy(bs_hbm, bs_v, in_sem.at[2])
    bs_in.start()
    q_in.start()
    prev_in.start()

    barrier = pltpu.get_barrier_semaphore()
    for s in range(1, W):
        pl.semaphore_signal(
            barrier,
            inc=1,
            device_id={"wall": lax.rem(w + s, W)},
            device_id_type=pl.DeviceIdType.MESH,
        )

    @pl.when(v > 0)
    def _():
        pl.semaphore_signal(
            barrier, inc=1, device_id={"vec": v - 1}, device_id_type=pl.DeviceIdType.MESH
        )

    @pl.when(v < V - 1)
    def _():
        pl.semaphore_signal(
            barrier, inc=1, device_id={"vec": v + 1}, device_id_type=pl.DeviceIdType.MESH
        )

    @pl.when(w == 0)
    def _():
        qpad[:, :, 0] = jnp.zeros((nvec, ncomp, nx, nz), jnp.float32)

    @pl.when(w == W - 1)
    def _():
        qpad[:, :, rows + 1] = jnp.zeros((nvec, ncomp, nx, nz), jnp.float32)

    one = jnp.ones((nx, nz), jnp.float32)

    def down_tables(r, carry):
        prod_d, prod_rho, beta = carry
        d = 1.0 - gap_s[r]
        p = 1.0 / (one * piv_s[r])
        rho = p * up_s[r]
        prod_d = prod_d * d
        weight = prod_rho * p
        tab_d[r] = prod_d
        tab_w[r] = weight
        tab_p[r] = p
        tab_rho[r] = rho
        return prod_d, prod_rho * rho, beta + weight * prod_d

    phi, psi, beta = lax.fori_loop(0, rows, down_tables, (one, one, one * 0.0))
    ctile[0] = phi[:, :128]
    ctile[1] = psi[:, :128]
    ctile[2] = beta[:, :128]

    def up_tables(t, carry):
        a, c = carry
        r = rows - 1 - t
        a = tab_p[r] * tab_d[r] + tab_rho[r] * a
        c = tab_rho[r] * c
        tab_a[r] = a
        tab_c[r] = c
        return a, c

    lax.fori_loop(0, rows, up_tables, (one * 0.0, one))

    neighbours = jnp.where(v > 0, 1, 0) + jnp.where(v < V - 1, 1, 0)
    pl.semaphore_wait(barrier, W - 1 + neighbours)

    def halo_up():
        return pltpu.make_async_remote_copy(
            src_ref=q_hbm.at[:, :, rows - 1],
            dst_ref=qpad.at[:, :, 0],
            send_sem=halo_send.at[0],
            recv_sem=halo_recv.at[0],
            device_id={"wall": w + 1},
            device_id_type=pl.DeviceIdType.MESH,
        )

    def halo_down():
        return pltpu.make_async_remote_copy(
            src_ref=q_hbm.at[:, :, 0],
            dst_ref=qpad.at[:, :, rows + 1],
            send_sem=halo_send.at[1],
            recv_sem=halo_recv.at[1],
            device_id={"wall": w - 1},
            device_id_type=pl.DeviceIdType.MESH,
        )

    def right_copy(k):
        part = pl.ds(k * CHUNK_ROWS, CHUNK_ROWS)
        return pltpu.make_async_remote_copy(
            src_ref=out_r.at[:, part],
            dst_ref=from_l.at[:, part],
            send_sem=lr_send.at[k],
            recv_sem=lr_recv.at[k],
            device_id={"vec": v + 1},
            device_id_type=pl.DeviceIdType.MESH,
        )

    def left_copy(k):
        part = pl.ds(k * CHUNK_ROWS, CHUNK_ROWS)
        return pltpu.make_async_remote_copy(
            src_ref=out_l.at[:, part],
            dst_ref=from_r.at[:, part],
            send_sem=rl_send.at[k],
            recv_sem=rl_recv.at[k],
            device_id={"vec": v - 1},
            device_id_type=pl.DeviceIdType.MESH,
        )

    def coef_copy(s):
        peer = lax.rem(w + s, W)
        return pltpu.make_async_remote_copy(
            src_ref=ctile,
            dst_ref=ctiles.at[w],
            send_sem=coef_send.at[s],
            recv_sem=coef_recv.at[W - s],
            device_id={"wall": peer},
            device_id_type=pl.DeviceIdType.MESH,
        )

    def coef_wait(s):
        pltpu.make_async_copy(ctile, ctiles.at[lax.rem(w + s, W)], coef_recv.at[s]).wait()

    slot = slots_s[lax.rem(step_s[0], slots_s.shape[0])]
    owner = lax.div(slot, stored)
    local = lax.rem(slot, stored)
    mine = owner == v
    before = owner < v
    shift = shift_s[0]

    def own_row(c, y):
        value = bs_v[0, c, y]
        for s in range(1, stored):
            value = jnp.where(local == s, bs_v[s, c, y], value)
        return value

    @pl.when(w < W - 1)
    def _():
        halo_up().start()

    @pl.when(w > 0)
    def _():
        halo_down().start()

    bs_in.wait()

    def each_row(k, body):
        def run(m, carry):
            body(lax.rem(m, ncomp), k * CHUNK_ROWS + lax.div(m, ncomp))
            return carry

        lax.fori_loop(0, ncomp * CHUNK_ROWS, run, 0)

    @pl.when(v == 0)
    def _():
        def go(k, carry):
            def put(c, y):
                out_r[c, y] = own_row(c, y)

            each_row(k, put)
            right_copy(k).start()
            return carry

        lax.fori_loop(0, chunks, go, 0)

    @pl.when(v == V - 1)
    def _():
        def go(k, carry):
            def put(c, y):
                out_l[c, y] = own_row(c, y)

            each_row(k, put)
            left_copy(k).start()
            return carry

        lax.fori_loop(0, chunks, go, 0)

    for s in range(1, W):
        coef_copy(s).start()

    q_in.wait()
    prev_in.wait()

    @pl.when(w < W - 1)
    def _():
        halo_down().wait_recv()

    @pl.when(w > 0)
    def _():
        halo_up().wait_recv()

    fcar[...] = jnp.zeros_like(fcar)
    bcar[...] = jnp.zeros_like(bcar)

    def compute_chunk(k):
        def row(m, carry):
            y = k * CHUNK_ROWS + m
            base = []
            for c in range(ncomp):
                got = jnp.where(before, from_l[c, y], from_r[c, y])
                got = jnp.where(mine, own_row(c, y), got).astype(jnp.float32)
                base.append(pltpu.roll(got, shift, 1))
            d = 1.0 - gap_s[y]
            weight = tab_w[y]

            def field(i, inner):
                n = lax.div(i, ncomp)
                c = lax.rem(i, ncomp)
                mid = qpad[n, c, y + 1]
                above = qpad[n, c, y + 2]
                below = qpad[n, c, y]
                dx = 0.5 * (pltpu.roll(mid, nx - 1, 0) - pltpu.roll(mid, 1, 0))
                dz = 0.5 * (pltpu.roll(mid, nz - 1, 1) - pltpu.roll(mid, 1, 1))
                explicit = -(base[0] * dx + base[1] * (0.5 * (above - below)) + base[2] * dz)
                expl[n, c, y] = explicit.astype(jnp.bfloat16)
                source = (
                    mid
                    + STEP_SIZE
                    * (NEW_WEIGHT * explicit + OLD_WEIGHT * prev_v[n, c, y].astype(jnp.float32))
                    + VISCOUS_WEIGHT * (above - 2.0 * mid + below)
                )
                swept = source + d * fcar[n, c]
                fcar[n, c] = swept
                bcar[n, c] = bcar[n, c] + weight * swept
                loc[n, c, y] = swept
                return inner

            lax.fori_loop(0, fields, field, 0)
            return carry

        lax.fori_loop(0, CHUNK_ROWS, row, 0)

    far = V - 1 - v

    def slot_step(t, carry):
        kl = t - HOP_LAG * v
        kr = t - HOP_LAG * far

        @pl.when((v > 0) & (kl >= 0) & (kl < chunks))
        def _():
            right_copy(kl).wait_recv()

            @pl.when(v < V - 1)
            def _():
                def put(c, y):
                    out_r[c, y] = jnp.where(mine, own_row(c, y), from_l[c, y])

                each_row(kl, put)
                right_copy(kl).start()

        @pl.when((v < V - 1) & (kr >= 0) & (kr < chunks))
        def _():
            left_copy(kr).wait_recv()

            @pl.when(v > 0)
            def _():
                def put(c, y):
                    out_l[c, y] = jnp.where(mine, own_row(c, y), from_r[c, y])

                each_row(kr, put)
                left_copy(kr).start()

        kc = jnp.minimum(kl, kr)

        @pl.when((kc >= 0) & (kc < chunks))
        def _():
            compute_chunk(kc)

        return carry

    lax.fori_loop(0, chunks + HOP_LAG * (V - 1), slot_step, 0)

    advec_out = pltpu.make_async_copy(expl, advec_hbm, out_sem.at[fields])
    advec_out.start()

    for s in range(1, W):
        coef_wait(s)
    ctiles[w] = ctile[...]

    def tail_response(m, total):
        j = W - 1 - m
        tile = ctiles[j]
        new = tile[2] + tile[1] * total * tile[0]
        return jnp.where(j > w, new, total)

    wide = nz // 128

    def widen(x):
        return jnp.concatenate([x] * wide, axis=-1)

    tail = widen(lax.fori_loop(0, W - 1, tail_response, jnp.zeros((nx, 128), jnp.float32)))
    gain = psi * tail

    def pack(i, carry):
        n = lax.div(i, ncomp)
        c = lax.rem(i, ncomp)
        f = fcar[n, c]
        fsend[n, c] = f.astype(jnp.bfloat16)
        esend[n, c] = (bcar[n, c] + gain * f).astype(jnp.bfloat16)
        return carry

    lax.fori_loop(0, fields, pack, 0)

    def carry_copy(s, src):
        return pltpu.make_async_remote_copy(
            src_ref=src,
            dst_ref=cin.at[w],
            send_sem=car_send.at[s],
            recv_sem=car_recv.at[W - s],
            device_id={"wall": lax.rem(w + s, W)},
            device_id_type=pl.DeviceIdType.MESH,
        )

    for s in range(1, W):

        @pl.when(w + s < W)
        def _():
            carry_copy(s, fsend).start()

        @pl.when(w + s >= W)
        def _():
            carry_copy(s, esend).start()

    def solve(i, carry):
        n = lax.div(i, ncomp)
        c = lax.rem(i, ncomp)
        later = jnp.zeros((nx, nz), jnp.float32)
        for y in range(rows - 1, -1, -1):
            later = tab_p[y] * loc[n, c, y] + tab_rho[y] * later
            loc[n, c, y] = later
        return carry

    lax.fori_loop(0, fields, solve, 0)

    for s in range(1, W):
        pltpu.make_async_copy(fsend, cin.at[lax.rem(w + s, W)], car_recv.at[s]).wait()

    def finish(i, carry):
        n = lax.div(i, ncomp)
        c = lax.rem(i, ncomp)

        def forward(j, total):
            tile = ctiles[j]
            new = cin[j, n, c].astype(jnp.float32) + widen(tile[0]) * total
            return jnp.where(j < w, new, total)

        def backward(m, total):
            j = W - 1 - m
            tile = ctiles[j]
            new = cin[j, n, c].astype(jnp.float32) + widen(tile[1]) * total
            return jnp.where(j > w, new, total)

        zero = jnp.zeros((nx, nz), jnp.float32)
        f_in = lax.fori_loop(0, W - 1, forward, zero)
        b_in = lax.fori_loop(0, W - 1, backward, zero)
        b_in = b_in + tail * (fcar[n, c] + phi * f_in)
        for y in range(rows):
            adv_v[n, c, y] = loc[n, c, y] + tab_a[y] * f_in + tab_c[y] * b_in
        pltpu.make_async_copy(adv_v.at[n, c], adv_hbm.at[n, c], out_sem.at[i]).start()
        return carry

    lax.fori_loop(0, fields, finish, 0)

    @pl.when(w < W - 1)
    def _():
        halo_up().wait_send()

    @pl.when(w > 0)
    def _():
        halo_down().wait_send()

    def drain(k, carry):
        @pl.when(v < V - 1)
        def _():
            right_copy(k).wait_send()

        @pl.when(v > 0)
        def _():
            left_copy(k).wait_send()

        return carry

    lax.fori_loop(0, chunks, drain, 0)
    for s in range(1, W):
        coef_copy(s).wait_send()
        carry_copy(s, fsend).wait_send()

    def drain_out(i, carry):
        n = lax.div(i, ncomp)
        c = lax.rem(i, ncomp)
        pltpu.make_async_copy(adv_v.at[n, c], adv_hbm.at[n, c], out_sem.at[i]).wait()
        return carry

    lax.fori_loop(0, fields, drain_out, 0)
    advec_out.wait()


def on_device(W, V, q, prev, bs, step, slots, shift, gap, piv, up):
    nvec, ncomp, rows, nx, nz = q.shape
    chunks = rows // CHUNK_ROWS
    field = (nvec, ncomp, rows, nx, nz)
    slab = (ncomp, rows, nx, nz)
    edge = (nvec, ncomp, nx, nz)
    any_spec = pl.BlockSpec(memory_space=pl.ANY)
    smem = pl.BlockSpec(memory_space=pltpu.SMEM)
    f32, bf16 = jnp.float32, jnp.bfloat16
    dma = pltpu.SemaphoreType.DMA
    return pl.pallas_call(
        functools.partial(kernel, W, V),
        out_shape=(jax.ShapeDtypeStruct(field, f32), jax.ShapeDtypeStruct(field, bf16)),
        in_specs=[any_spec] * 3 + [smem] * 6,
        out_specs=(any_spec, any_spec),
        scratch_shapes=[
            pltpu.VMEM((nvec, ncomp, rows + 2, nx, nz), f32),
            pltpu.VMEM(field, bf16),
            pltpu.VMEM(bs.shape, bf16),
            pltpu.VMEM(slab, bf16),
            pltpu.VMEM(slab, bf16),
            pltpu.VMEM(slab, bf16),
            pltpu.VMEM(slab, bf16),
            pltpu.VMEM(field, f32),
            pltpu.VMEM(field, bf16),
            pltpu.VMEM(field, f32),
            pltpu.VMEM(edge, f32),
            pltpu.VMEM(edge, f32),
            pltpu.VMEM(edge, bf16),
            pltpu.VMEM(edge, bf16),
            pltpu.VMEM((W,) + edge, bf16),
            pltpu.VMEM((3, nx, 128), f32),
            pltpu.VMEM((W, 3, nx, 128), f32),
        ]
        + [pltpu.VMEM((rows, nx, nz), f32)] * 6
        + [
            dma((3,)),
            dma((2,)),
            dma((2,)),
            dma((W,)),
            dma((W,)),
            dma((chunks,)),
            dma((chunks,)),
            dma((chunks,)),
            dma((chunks,)),
            dma((W,)),
            dma((W,)),
            dma((nvec * ncomp + 1,)),
        ],
        compiler_params=pltpu.CompilerParams(
            collective_id=0, has_side_effects=True, vmem_limit_bytes=48 * 1024 * 1024
        ),
    )(q, prev, bs, step, slots, shift, gap, piv, up)


def solution(mesh):
    W, V = mesh.shape["wall"], mesh.shape["vec"]
    field = P("vec", None, "wall", None, None)
    return jax.shard_map(
        functools.partial(on_device, W, V),
        mesh=mesh,
        in_specs=(field, field, field, P(), P(), P(), P("wall"), P("wall"), P("wall")),
        out_specs=(field, field),
        check_vma=False,
    )
```

time: 99.6 us -> 39 us (0.39)
  blocking collectives: 34.9 us -> 0 us
  Pallas kernels: 0 us -> 31.8 us
  other arithmetic: 19.5 us -> 0 us
  between operations: 19 us -> 2.04 us
  local copies, waits for them, and re-layouts: 16.7 us -> 4.88 us
  starting transfers between devices: 4.99 us -> 0 us
  matrix products: 3.7 us -> 0 us
    pallas_call x0 -> x1, Pallas kernels: none -> 31.8 us  [on_device(): pl.pallas_call(functools.partial(kernel, W, V), out_shape=(jax.ShapeDtype...]
    all_gather x2 -> x0, blocking collectives: 19.2 us -> none  [the longest x1 11 us: on_device(): lax.all_gather(forward_value[None], 'wall', axis=0, tiled=True)]
    unnamed x1 -> x0, blocking collectives: 15.7 us -> none
    reduce_prod x6 -> x0, other arithmetic: 5.78 us -> none  [the longest x1 1.36 us: on_device(): jnp.prod(jnp.where((middle_dev > source_dev) & (middle_dev < own_index),...]
    ppermute x2 -> x0, starting transfers between devices: 4.95 us -> none  [the longest x1 3.67 us: padded_2(): lax.ppermute(tail, axis, [(i, (i + 1) % count) for i in range(ends)])]
    slice x9 -> x0, local copies, waits for them, and re-layouts: 4.73 us -> none  [the longest x4 3.02 us: periodic_diff(): return 0.5 * (jnp.roll(field, -1, along) - jnp.roll(field, 1, along))]
    convert_element_type x2 -> x0, other arithmetic: 3.83 us -> none  [the longest x1 2.52 us: on_device(): advection = explicit.astype(jnp.bfloat16)]
    dot_general x4 -> x0, matrix products: 3.7 us -> none  [the longest x2 2.59 us: apply_rows(): jnp.einsum('ji,vcixz->vcjxz', matrix, values, precision=lax.Precision.HIG...]
  transfers between devices with their start and end apart: 3 -> 0, of which waited for: 0 -> 0; matrix products, arithmetic and copies ran while one was open for 28% -> 0% of each run, Pallas kernels for 0% -> 0%
where the time goes in v1:
time: 39 us; the launch traced here: 38.7 us
  Pallas kernels  31.8 us (82%)
  local copies, waits for them, and re-layouts  4.88 us (13%)
  between operations  2.04 us (5%)
    pallas_call x1, Pallas kernels, on_device(): pl.pallas_call(functools.partial(kernel, W, V), out_shape=(jax.ShapeDtype...  31.8 us
    unnamed x16, local copies, waits for them, and re-layouts  4.88 us

profile of v1, /device:TPU:0, one launch (start us, length us, event | category | flops | bytes accessed | tf_op | source)
XLA Modules:
  0.0 38.7 jit_solution(6557922648853261924)
XLA Ops:
  0.6 0.0 copy-start.6
  1.3 0.0 copy-start.3
  1.3 0.0 copy-start.4
  1.3 0.0 copy-start.5
  2.0 0.0 copy-done.6
  2.0 0.0 copy-done.3
  2.0 0.0 copy-done.4
  2.0 0.0 copy-done.5
  2.0 0.0 copy-start
  2.1 1.2 %copy-done = f32[2,3,12,8,384]{4,3,2,1,0:T(8,128)S(1)} copy-done((f32[2,3,12,8,384]{4,3,2,1,0:T(8,128)S(1)}, f32[2,3,12,8,384]{4,3,2,1,0:T(8,128)}, u32[]{:S(2)}) %copy-start) | copy-done | bytes 884760
  3.2 0.0 copy-start.1
  3.2 1.0 %copy-done.1 = bf16[2,3,12,8,384]{4,3,2,1,0:T(8,128)(2,1)S(1)} copy-done((bf16[2,3,12,8,384]{4,3,2,1,0:T(8,128)(2,1)S(1)}, bf16[2,3,12,8,384]{4,3,2,1,0:T(8,128)(2,1)}, u32[]{:S(2)}) %copy-start.1) | copy-done | bytes 442392
  4.2 0.0 copy-start.2
  4.2 1.0 %copy-done.2 = bf16[2,3,12,8,384]{4,3,2,1,0:T(8,128)(2,1)S(1)} copy-done((bf16[2,3,12,8,384]{4,3,2,1,0:T(8,128)(2,1)S(1)}, bf16[2,3,12,8,384]{4,3,2,1,0:T(8,128)(2,1)}, u32[]{:S(2)}) %copy-start.2) | copy-done | bytes 442392
  5.2 31.8 %shard_map.104 = (f32[2,3,12,8,384]{4,3,2,1,0:T(8,128)S(1)}, bf16[2,3,12,8,384]{4,3,2,1,0:T(8,128)(2,1)S(1)}) custom-call(f32[2,3,12,8,384]{4,3,2,1,0:T(8,128)S(1)} %copy-done, bf16[2,3,12,8,384]{4,3,2,1,0:T(8,128)(2,1)S(1)} %copy-done.1, bf16[2,3,12,8,384]{4,3,2,1,0:T(8,128)(2,1)S(1)} %copy-done.2, s32[1]{0:T(128)S(6)} %copy.13.step_s, s32[8]{0:T(128)S(1)} %copy-done.3, ...), custom_call_target="tpu_custom_call" | custom-call | tf_op jit(solution)/shard_map/pallas_call | solution.py:485
  37.0 0.9 %copy.15 = f32[2,3,12,8,384]{4,3,2,1,0:T(8,128)} copy(f32[2,3,12,8,384]{4,3,2,1,0:T(8,128)S(1)} %get-tuple-element.4) | data formatting | bytes 1769472
  37.9 0.8 %copy.16 = bf16[2,3,12,8,384]{4,3,2,1,0:T(8,128)(2,1)} copy(bf16[2,3,12,8,384]{4,3,2,1,0:T(8,128)(2,1)S(1)} %get-tuple-element.5) | data formatting | bytes 884736
Async XLA Ops:
  0.6 1.4 %copy-start.6 = (f32[12]{0:T(128)S(1)}, f32[12]{0:T(128)}, u32[]{:S(2)}) copy-start(f32[12]{0:T(128)} %up_s.1) | copy-start | bytes 148
  1.3 0.7 %copy-start.3 = (s32[8]{0:T(128)S(1)}, s32[8]{0:T(128)}, u32[]{:S(2)}) copy-start(s32[8]{0:T(128)} %slots_s.1) | copy-start | bytes 100
  1.3 0.7 %copy-start.4 = (f32[12]{0:T(128)S(1)}, f32[12]{0:T(128)}, u32[]{:S(2)}) copy-start(f32[12]{0:T(128)} %gap_s.1) | copy-start | bytes 148
  1.3 0.7 %copy-start.5 = (f32[12]{0:T(128)S(1)}, f32[12]{0:T(128)}, u32[]{:S(2)}) copy-start(f32[12]{0:T(128)} %piv_s.1) | copy-start | bytes 148
  2.0 1.2 %copy-start = (f32[2,3,12,8,384]{4,3,2,1,0:T(8,128)S(1)}, f32[2,3,12,8,384]{4,3,2,1,0:T(8,128)}, u32[]{:S(2)}) copy-start(f32[2,3,12,8,384]{4,3,2,1,0:T(8,128)} %q_hbm.1) | copy-start | bytes 2654212
  3.2 1.0 %copy-start.1 = (bf16[2,3,12,8,384]{4,3,2,1,0:T(8,128)(2,1)S(1)}, bf16[2,3,12,8,384]{4,3,2,1,0:T(8,128)(2,1)}, u32[]{:S(2)}) copy-start(bf16[2,3,12,8,384]{4,3,2,1,0:T(8,128)(2,1)} %prev_hbm.1) | copy-start | bytes 1327108
  4.2 1.0 %copy-start.2 = (bf16[2,3,12,8,384]{4,3,2,1,0:T(8,128)(2,1)S(1)}, bf16[2,3,12,8,384]{4,3,2,1,0:T(8,128)(2,1)}, u32[]{:S(2)}) copy-start(bf16[2,3,12,8,384]{4,3,2,1,0:T(8,128)(2,1)} %bs_hbm.1) | copy-start | bytes 1327108

commit v2 on v1

--- a/solution.py
+++ b/solution.py
@@ -21,14 +21,26 @@
     q_hbm,
     prev_hbm,
     bs_hbm,
+    step_h,
+    slots_h,
+    shift_h,
+    gap_h,
+    piv_h,
+    up_h,
+    adv_hbm,
+    advec_hbm,
     step_s,
     slots_s,
     shift_s,
     gap_s,
     piv_s,
     up_s,
-    adv_hbm,
-    advec_hbm,
+    dx_v,
+    dy_v,
+    dz_v,
+    own_v,
+    tab_f,
+    tab_b,
     qpad,
     prev_v,
     bs_v,
@@ -53,6 +65,7 @@
     tab_a,
     tab_c,
     in_sem,
+    small_sem,
     halo_send,
     halo_recv,
     coef_send,
@@ -75,6 +88,21 @@
     q_in = pltpu.make_async_copy(q_hbm, qpad.at[:, :, pl.ds(1, rows)], in_sem.at[0])
     prev_in = pltpu.make_async_copy(prev_hbm, prev_v, in_sem.at[1])
     bs_in = pltpu.make_async_copy(bs_hbm, bs_v, in_sem.at[2])
+    small = [
+        pltpu.make_async_copy(src, dst, small_sem.at[n])
+        for n, (src, dst) in enumerate(
+            (
+                (step_h, step_s),
+                (slots_h, slots_s),
+                (shift_h, shift_s),
+                (gap_h, gap_s),
+                (piv_h, piv_s),
+                (up_h, up_s),
+            )
+        )
+    ]
+    for copy in small:
+        copy.start()
     bs_in.start()
     q_in.start()
     prev_in.start()
@@ -107,6 +135,9 @@
     @pl.when(w == W - 1)
     def _():
         qpad[:, :, rows + 1] = jnp.zeros((nvec, ncomp, nx, nz), jnp.float32)
+
+    for copy in small:
+        copy.wait()
 
     one = jnp.ones((nx, nz), jnp.float32)
 
@@ -162,10 +193,10 @@
             device_id_type=pl.DeviceIdType.MESH,
         )
 
-    def right_copy(k):
+    def right_copy(k, src):
         part = pl.ds(k * CHUNK_ROWS, CHUNK_ROWS)
         return pltpu.make_async_remote_copy(
-            src_ref=out_r.at[:, part],
+            src_ref=src.at[:, part],
             dst_ref=from_l.at[:, part],
             send_sem=lr_send.at[k],
             recv_sem=lr_recv.at[k],
@@ -173,10 +204,10 @@
             device_id_type=pl.DeviceIdType.MESH,
         )
 
-    def left_copy(k):
+    def left_copy(k, src):
         part = pl.ds(k * CHUNK_ROWS, CHUNK_ROWS)
         return pltpu.make_async_remote_copy(
-            src_ref=out_l.at[:, part],
+            src_ref=src.at[:, part],
             dst_ref=from_r.at[:, part],
             send_sem=rl_send.at[k],
             recv_sem=rl_recv.at[k],
@@ -222,35 +253,28 @@
     bs_in.wait()
 
     def each_row(k, body):
-        def run(m, carry):
-            body(lax.rem(m, ncomp), k * CHUNK_ROWS + lax.div(m, ncomp))
-            return carry
-
-        lax.fori_loop(0, ncomp * CHUNK_ROWS, run, 0)
-
-    @pl.when(v == 0)
-    def _():
-        def go(k, carry):
-            def put(c, y):
-                out_r[c, y] = own_row(c, y)
-
-            each_row(k, put)
-            right_copy(k).start()
-            return carry
-
-        lax.fori_loop(0, chunks, go, 0)
-
-    @pl.when(v == V - 1)
-    def _():
-        def go(k, carry):
-            def put(c, y):
-                out_l[c, y] = own_row(c, y)
-
-            each_row(k, put)
-            left_copy(k).start()
-            return carry
-
-        lax.fori_loop(0, chunks, go, 0)
+        for m in range(CHUNK_ROWS):
+            for c in range(ncomp):
+                body(c, k * CHUNK_ROWS + m)
+
+    def shift_own(k, carry):
+        def put(c, y):
+            row = pltpu.roll(own_row(c, y).astype(jnp.float32), shift, 1)
+            own_v[c, y] = row.astype(jnp.bfloat16)
+
+        each_row(k, put)
+
+        @pl.when(v == 0)
+        def _():
+            right_copy(k, own_v).start()
+
+        @pl.when(v == V - 1)
+        def _():
+            left_copy(k, own_v).start()
+
+        return carry
+
+    lax.fori_loop(0, chunks, shift_own, 0)
 
     for s in range(1, W):
         coef_copy(s).start()
@@ -258,6 +282,31 @@
     q_in.wait()
     prev_in.wait()
 
+    def prepare(n, c, y):
+        mid = qpad[n, c, y + 1]
+        above = qpad[n, c, y + 2]
+        below = qpad[n, c, y]
+        dx_v[n, c, y] = 0.5 * (pltpu.roll(mid, nx - 1, 0) - pltpu.roll(mid, 1, 0))
+        dz_v[n, c, y] = 0.5 * (pltpu.roll(mid, nz - 1, 1) - pltpu.roll(mid, 1, 1))
+        dy_v[n, c, y] = 0.5 * (above - below)
+        loc[n, c, y] = (
+            mid
+            + (STEP_SIZE * OLD_WEIGHT) * prev_v[n, c, y].astype(jnp.float32)
+            + VISCOUS_WEIGHT * (above - 2.0 * mid + below)
+        )
+
+    def prepare_inner(i, carry):
+        for y in range(1, rows - 1):
+            prepare(lax.div(i, ncomp), lax.rem(i, ncomp), y)
+        return carry
+
+    def prepare_edges(i, carry):
+        for y in (0, rows - 1):
+            prepare(lax.div(i, ncomp), lax.rem(i, ncomp), y)
+        return carry
+
+    lax.fori_loop(0, fields, prepare_inner, 0)
+
     @pl.when(w < W - 1)
     def _():
         halo_down().wait_recv()
@@ -265,47 +314,32 @@
     @pl.when(w > 0)
     def _():
         halo_up().wait_recv()
+
+    lax.fori_loop(0, fields, prepare_edges, 0)
 
     fcar[...] = jnp.zeros_like(fcar)
     bcar[...] = jnp.zeros_like(bcar)
 
     def compute_chunk(k):
-        def row(m, carry):
+        for m in range(CHUNK_ROWS):
             y = k * CHUNK_ROWS + m
             base = []
             for c in range(ncomp):
                 got = jnp.where(before, from_l[c, y], from_r[c, y])
-                got = jnp.where(mine, own_row(c, y), got).astype(jnp.float32)
-                base.append(pltpu.roll(got, shift, 1))
+                base.append(jnp.where(mine, own_v[c, y], got).astype(jnp.float32))
             d = 1.0 - gap_s[y]
             weight = tab_w[y]
-
-            def field(i, inner):
-                n = lax.div(i, ncomp)
-                c = lax.rem(i, ncomp)
-                mid = qpad[n, c, y + 1]
-                above = qpad[n, c, y + 2]
-                below = qpad[n, c, y]
-                dx = 0.5 * (pltpu.roll(mid, nx - 1, 0) - pltpu.roll(mid, 1, 0))
-                dz = 0.5 * (pltpu.roll(mid, nz - 1, 1) - pltpu.roll(mid, 1, 1))
-                explicit = -(base[0] * dx + base[1] * (0.5 * (above - below)) + base[2] * dz)
-                expl[n, c, y] = explicit.astype(jnp.bfloat16)
-                source = (
-                    mid
-                    + STEP_SIZE
-                    * (NEW_WEIGHT * explicit + OLD_WEIGHT * prev_v[n, c, y].astype(jnp.float32))
-                    + VISCOUS_WEIGHT * (above - 2.0 * mid + below)
-                )
-                swept = source + d * fcar[n, c]
-                fcar[n, c] = swept
-                bcar[n, c] = bcar[n, c] + weight * swept
-                loc[n, c, y] = swept
-                return inner
-
-            lax.fori_loop(0, fields, field, 0)
-            return carry
-
-        lax.fori_loop(0, CHUNK_ROWS, row, 0)
+            for n in range(nvec):
+                for c in range(ncomp):
+                    explicit = -(
+                        base[0] * dx_v[n, c, y] + base[1] * dy_v[n, c, y] + base[2] * dz_v[n, c, y]
+                    )
+                    expl[n, c, y] = explicit.astype(jnp.bfloat16)
+                    source = loc[n, c, y] + (STEP_SIZE * NEW_WEIGHT) * explicit
+                    swept = source + d * fcar[n, c]
+                    fcar[n, c] = swept
+                    bcar[n, c] = bcar[n, c] + weight * swept
+                    loc[n, c, y] = swept
 
     far = V - 1 - v
 
@@ -315,27 +349,27 @@
 
         @pl.when((v > 0) & (kl >= 0) & (kl < chunks))
         def _():
-            right_copy(kl).wait_recv()
+            right_copy(kl, own_v).wait_recv()
 
             @pl.when(v < V - 1)
             def _():
                 def put(c, y):
-                    out_r[c, y] = jnp.where(mine, own_row(c, y), from_l[c, y])
+                    out_r[c, y] = jnp.where(mine, own_v[c, y], from_l[c, y])
 
                 each_row(kl, put)
-                right_copy(kl).start()
+                right_copy(kl, out_r).start()
 
         @pl.when((v < V - 1) & (kr >= 0) & (kr < chunks))
         def _():
-            left_copy(kr).wait_recv()
+            left_copy(kr, own_v).wait_recv()
 
             @pl.when(v > 0)
             def _():
                 def put(c, y):
-                    out_l[c, y] = jnp.where(mine, own_row(c, y), from_r[c, y])
+                    out_l[c, y] = jnp.where(mine, own_v[c, y], from_r[c, y])
 
                 each_row(kr, put)
-                left_copy(kr).start()
+                left_copy(kr, out_l).start()
 
         kc = jnp.minimum(kl, kr)
 
@@ -352,7 +386,6 @@
 
     for s in range(1, W):
         coef_wait(s)
-    ctiles[w] = ctile[...]
 
     def tail_response(m, total):
         j = W - 1 - m
@@ -368,15 +401,11 @@
     tail = widen(lax.fori_loop(0, W - 1, tail_response, jnp.zeros((nx, 128), jnp.float32)))
     gain = psi * tail
 
-    def pack(i, carry):
-        n = lax.div(i, ncomp)
-        c = lax.rem(i, ncomp)
-        f = fcar[n, c]
-        fsend[n, c] = f.astype(jnp.bfloat16)
-        esend[n, c] = (bcar[n, c] + gain * f).astype(jnp.bfloat16)
-        return carry
-
-    lax.fori_loop(0, fields, pack, 0)
+    for n in range(nvec):
+        for c in range(ncomp):
+            f = fcar[n, c]
+            fsend[n, c] = f.astype(jnp.bfloat16)
+            esend[n, c] = (bcar[n, c] + gain * f).astype(jnp.bfloat16)
 
     def carry_copy(s, src):
         return pltpu.make_async_remote_copy(
@@ -409,28 +438,44 @@
 
     lax.fori_loop(0, fields, solve, 0)
 
-    for s in range(1, W):
-        pltpu.make_async_copy(fsend, cin.at[lax.rem(w + s, W)], car_recv.at[s]).wait()
+    def forward_weight(m, prod):
+        j = w - 1 - m
+        tab_f[j] = prod
+        return prod * widen(ctiles[j, 0])
+
+    def backward_weight(m, prod):
+        j = w + 1 + m
+        tab_b[j] = prod
+        return prod * widen(ctiles[j, 1])
+
+    tab_f[...] = jnp.zeros_like(tab_f)
+    tab_b[...] = jnp.zeros_like(tab_b)
+    lax.fori_loop(0, w, forward_weight, one)
+    lax.fori_loop(0, W - 1 - w, backward_weight, one)
+
+    pairs = [(n, c) for n in range(nvec) for c in range(ncomp)]
+
+    def gather(s, sums):
+        j = lax.rem(w + s, W)
+        pltpu.make_async_copy(fsend, cin.at[j], car_recv.at[s]).wait()
+        wf, wb = tab_f[j], tab_b[j]
+        new = []
+        for (n, c), (f_in, b_in) in zip(pairs, sums):
+            value = cin[j, n, c].astype(jnp.float32)
+            new.append((f_in + wf * value, b_in + wb * value))
+        return tuple(new)
+
+    sums = tuple((one * 0.0, one * 0.0) for _ in pairs)
+    sums = lax.fori_loop(1, W, gather, sums)
+    for (n, c), (f_in, b_in) in zip(pairs, sums):
+        bcar[n, c] = b_in + tail * (fcar[n, c] + phi * f_in)
+        fcar[n, c] = f_in
 
     def finish(i, carry):
         n = lax.div(i, ncomp)
         c = lax.rem(i, ncomp)
-
-        def forward(j, total):
-            tile = ctiles[j]
-            new = cin[j, n, c].astype(jnp.float32) + widen(tile[0]) * total
-            return jnp.where(j < w, new, total)
-
-        def backward(m, total):
-            j = W - 1 - m
-            tile = ctiles[j]
-            new = cin[j, n, c].astype(jnp.float32) + widen(tile[1]) * total
-            return jnp.where(j > w, new, total)
-
-        zero = jnp.zeros((nx, nz), jnp.float32)
-        f_in = lax.fori_loop(0, W - 1, forward, zero)
-        b_in = lax.fori_loop(0, W - 1, backward, zero)
-        b_in = b_in + tail * (fcar[n, c] + phi * f_in)
+        f_in = fcar[n, c]
+        b_in = bcar[n, c]
         for y in range(rows):
             adv_v[n, c, y] = loc[n, c, y] + tab_a[y] * f_in + tab_c[y] * b_in
         pltpu.make_async_copy(adv_v.at[n, c], adv_hbm.at[n, c], out_sem.at[i]).start()
@@ -449,11 +494,11 @@
     def drain(k, carry):
         @pl.when(v < V - 1)
         def _():
-            right_copy(k).wait_send()
+            right_copy(k, own_v).wait_send()
 
         @pl.when(v > 0)
         def _():
-            left_copy(k).wait_send()
+            left_copy(k, own_v).wait_send()
 
         return carry
 
@@ -479,15 +524,27 @@
     slab = (ncomp, rows, nx, nz)
     edge = (nvec, ncomp, nx, nz)
     any_spec = pl.BlockSpec(memory_space=pl.ANY)
-    smem = pl.BlockSpec(memory_space=pltpu.SMEM)
+    hbm = pl.BlockSpec(memory_space=pltpu.HBM)
     f32, bf16 = jnp.float32, jnp.bfloat16
     dma = pltpu.SemaphoreType.DMA
     return pl.pallas_call(
         functools.partial(kernel, W, V),
         out_shape=(jax.ShapeDtypeStruct(field, f32), jax.ShapeDtypeStruct(field, bf16)),
-        in_specs=[any_spec] * 3 + [smem] * 6,
+        in_specs=[hbm] * 9,
         out_specs=(any_spec, any_spec),
         scratch_shapes=[
+            pltpu.SMEM(step.shape, step.dtype),
+            pltpu.SMEM(slots.shape, slots.dtype),
+            pltpu.SMEM(shift.shape, shift.dtype),
+            pltpu.SMEM(gap.shape, gap.dtype),
+            pltpu.SMEM(piv.shape, piv.dtype),
+            pltpu.SMEM(up.shape, up.dtype),
+            pltpu.VMEM(field, f32),
+            pltpu.VMEM(field, f32),
+            pltpu.VMEM(field, f32),
+            pltpu.VMEM(slab, bf16),
+            pltpu.VMEM((W, nx, nz), f32),
+            pltpu.VMEM((W, nx, nz), f32),
             pltpu.VMEM((nvec, ncomp, rows + 2, nx, nz), f32),
             pltpu.VMEM(field, bf16),
             pltpu.VMEM(bs.shape, bf16),
@@ -509,6 +566,7 @@
         + [pltpu.VMEM((rows, nx, nz), f32)] * 6
         + [
             dma((3,)),
+            dma((6,)),
             dma((2,)),
             dma((2,)),
             dma((W,)),
@@ -522,7 +580,7 @@
             dma((nvec * ncomp + 1,)),
         ],
         compiler_params=pltpu.CompilerParams(
-            collective_id=0, has_side_effects=True, vmem_limit_bytes=48 * 1024 * 1024
+            collective_id=0, has_side_effects=True, vmem_limit_bytes=63 * 1024 * 1024
         ),
     )(q, prev, bs, step, slots, shift, gap, piv, up)
 

time: 39 us -> 32.1 us (0.82)
  Pallas kernels: 31.8 us -> 27.1 us
  local copies, waits for them, and re-layouts: 4.88 us -> 2.95 us
    pallas_call x1, Pallas kernels: 31.8 us -> 27.1 us  [on_device(): pl.pallas_call(functools.partial(kernel, W, V), out_shape=(jax.ShapeDtype...]
    unnamed x16 -> x4, local copies, waits for them, and re-layouts: 4.88 us -> 2.95 us
where the time goes in v2:
time: 32.1 us; the launch traced here: 32 us
  Pallas kernels  27.1 us (84%)
  local copies, waits for them, and re-layouts  2.95 us (9%)
  between operations  1.94 us (6%)
    pallas_call x1, Pallas kernels, on_device(): pl.pallas_call(functools.partial(kernel, W, V), out_shape=(jax.ShapeDtype...  27.1 us
    unnamed x4, local copies, waits for them, and re-layouts  2.95 us

profile of v2, /device:TPU:0, one launch (start us, length us, event | category | flops | bytes accessed | tf_op | source)
XLA Modules:
  0.0 32.0 jit_solution(5763487201165561748)
XLA Ops:
  1.9 27.1 %shard_map.104 = (f32[2,3,12,8,384]{4,3,2,1,0:T(8,128)}, bf16[2,3,12,8,384]{4,3,2,1,0:T(8,128)(2,1)}) custom-call(f32[2,3,12,8,384]{4,3,2,1,0:T(8,128)} %q_hbm.1, bf16[2,3,12,8,384]{4,3,2,1,0:T(8,128)(2,1)} %prev_hbm.1, bf16[2,3,12,8,384]{4,3,2,1,0:T(8,128)(2,1)} %bs_hbm.1, s32[1]{0:T(128)S(6)} %copy.13.step_h, s32[8]{0:T(128)} %slots_h.1, ...), custom_call_target="tpu_custom_call" | custom-call | tf_op jit(solution)/shard_map/pallas_call | solution.py:530
  29.0 0.0 copy-start
  29.0 2.2 %copy.15 = f32[2,3,12,8,384]{4,3,2,1,0:T(8,128)} copy(f32[2,3,12,8,384]{4,3,2,1,0:T(8,128)} %get-tuple-element.4) | data formatting | bytes 1769472
  31.2 0.0 copy-done
  31.2 0.8 %copy.16 = bf16[2,3,12,8,384]{4,3,2,1,0:T(8,128)(2,1)} copy(bf16[2,3,12,8,384]{4,3,2,1,0:T(8,128)(2,1)S(1)} %copy-done) | data formatting | bytes 884736
Async XLA Ops:
  29.0 2.2 %copy-start = (bf16[2,3,12,8,384]{4,3,2,1,0:T(8,128)(2,1)S(1)}, bf16[2,3,12,8,384]{4,3,2,1,0:T(8,128)(2,1)}, u32[]{:S(2)}) copy-start(bf16[2,3,12,8,384]{4,3,2,1,0:T(8,128)(2,1)} %get-tuple-element.5) | copy-start | bytes 1327108

commit v3 on v2

--- a/solution.py
+++ b/solution.py
@@ -12,7 +12,8 @@
 OLD_WEIGHT = -17.0 / 60.0
 VISCOUS_WEIGHT = -0.06
 CHUNK_ROWS = 2
-HOP_LAG = 2
+HOP_LAG = 3
+PREP_UNROLL = 2
 
 
 def kernel(
@@ -295,27 +296,21 @@
             + VISCOUS_WEIGHT * (above - 2.0 * mid + below)
         )
 
-    def prepare_inner(i, carry):
-        for y in range(1, rows - 1):
-            prepare(lax.div(i, ncomp), lax.rem(i, ncomp), y)
-        return carry
-
-    def prepare_edges(i, carry):
-        for y in (0, rows - 1):
-            prepare(lax.div(i, ncomp), lax.rem(i, ncomp), y)
-        return carry
-
-    lax.fori_loop(0, fields, prepare_inner, 0)
-
-    @pl.when(w < W - 1)
-    def _():
-        halo_down().wait_recv()
-
-    @pl.when(w > 0)
-    def _():
-        halo_up().wait_recv()
-
-    lax.fori_loop(0, fields, prepare_edges, 0)
+    def prepare_chunk(p):
+        def run(i, carry):
+            for m in range(CHUNK_ROWS):
+                prepare(lax.div(i, ncomp), lax.rem(i, ncomp), p * CHUNK_ROWS + m)
+            return carry
+
+        @pl.when((p == 0) & (w > 0))
+        def _():
+            halo_up().wait_recv()
+
+        @pl.when((p == chunks - 1) & (w < W - 1))
+        def _():
+            halo_down().wait_recv()
+
+        lax.fori_loop(0, fields, run, 0, unroll=PREP_UNROLL)
 
     fcar[...] = jnp.zeros_like(fcar)
     bcar[...] = jnp.zeros_like(bcar)
@@ -370,6 +365,10 @@
 
                 each_row(kr, put)
                 left_copy(kr, out_l).start()
+
+        @pl.when(t < chunks)
+        def _():
+            prepare_chunk(jnp.where(t < 2, t + 1, jnp.where(t == 2, 0, t)))
 
         kc = jnp.minimum(kl, kr)
 

time: 32.1 us -> 28.8 us (0.90)
  Pallas kernels: 27.1 us -> 23.8 us
    pallas_call x1, Pallas kernels: 27.1 us -> 23.8 us  [on_device(): pl.pallas_call(functools.partial(kernel, W, V), out_shape=(jax.ShapeDtype...]
where the time goes in v3:
time: 28.8 us; the launch traced here: 28.7 us
  Pallas kernels  23.8 us (83%)
  local copies, waits for them, and re-layouts  2.95 us (10%)
  between operations  1.94 us (7%)
    pallas_call x1, Pallas kernels, on_device(): pl.pallas_call(functools.partial(kernel, W, V), out_shape=(jax.ShapeDtype...  23.8 us
    unnamed x4, local copies, waits for them, and re-layouts  2.95 us

profile of v3, /device:TPU:0, one launch (start us, length us, event | category | flops | bytes accessed | tf_op | source)
XLA Modules:
  0.0 28.7 jit_solution(18247839461443404829)
XLA Ops:
  1.9 23.8 %shard_map.104 = (f32[2,3,12,8,384]{4,3,2,1,0:T(8,128)}, bf16[2,3,12,8,384]{4,3,2,1,0:T(8,128)(2,1)}) custom-call(f32[2,3,12,8,384]{4,3,2,1,0:T(8,128)} %q_hbm.1, bf16[2,3,12,8,384]{4,3,2,1,0:T(8,128)(2,1)} %prev_hbm.1, bf16[2,3,12,8,384]{4,3,2,1,0:T(8,128)(2,1)} %bs_hbm.1, s32[1]{0:T(128)S(6)} %copy.13.step_h, s32[8]{0:T(128)} %slots_h.1, ...), custom_call_target="tpu_custom_call" | custom-call | tf_op jit(solution)/shard_map/pallas_call | solution.py:529
  25.7 0.0 copy-start
  25.7 2.2 %copy.15 = f32[2,3,12,8,384]{4,3,2,1,0:T(8,128)} copy(f32[2,3,12,8,384]{4,3,2,1,0:T(8,128)} %get-tuple-element.4) | data formatting | bytes 1769472
  27.9 0.0 copy-done
  27.9 0.8 %copy.16 = bf16[2,3,12,8,384]{4,3,2,1,0:T(8,128)(2,1)} copy(bf16[2,3,12,8,384]{4,3,2,1,0:T(8,128)(2,1)S(1)} %copy-done) | data formatting | bytes 884736
Async XLA Ops:
  25.7 2.2 %copy-start = (bf16[2,3,12,8,384]{4,3,2,1,0:T(8,128)(2,1)S(1)}, bf16[2,3,12,8,384]{4,3,2,1,0:T(8,128)(2,1)}, u32[]{:S(2)}) copy-start(bf16[2,3,12,8,384]{4,3,2,1,0:T(8,128)(2,1)} %get-tuple-element.5) | copy-start | bytes 1327108

commit v4 on v3

--- a/solution.py
+++ b/solution.py
@@ -28,8 +28,12 @@
     gap_h,
     piv_h,
     up_h,
-    adv_hbm,
+    part_hbm,
     advec_hbm,
+    f_hbm,
+    b_hbm,
+    a_hbm,
+    c_hbm,
     step_s,
     slots_s,
     shift_s,
@@ -51,7 +55,7 @@
     out_l,
     loc,
     expl,
-    adv_v,
+    edges,
     fcar,
     bcar,
     fsend,
@@ -63,8 +67,7 @@
     tab_w,
     tab_p,
     tab_rho,
-    tab_a,
-    tab_c,
+    tabs,
     in_sem,
     small_sem,
     halo_send,
@@ -165,8 +168,8 @@
         r = rows - 1 - t
         a = tab_p[r] * tab_d[r] + tab_rho[r] * a
         c = tab_rho[r] * c
-        tab_a[r] = a
-        tab_c[r] = c
+        tabs[0, r] = a
+        tabs[1, r] = c
         return a, c
 
     lax.fori_loop(0, rows, up_tables, (one * 0.0, one))
@@ -382,6 +385,10 @@
 
     advec_out = pltpu.make_async_copy(expl, advec_hbm, out_sem.at[fields])
     advec_out.start()
+    a_out = pltpu.make_async_copy(tabs.at[0], a_hbm, out_sem.at[fields + 3])
+    a_out.start()
+    c_out = pltpu.make_async_copy(tabs.at[1], c_hbm, out_sem.at[fields + 4])
+    c_out.start()
 
     for s in range(1, W):
         coef_wait(s)
@@ -433,6 +440,7 @@
         for y in range(rows - 1, -1, -1):
             later = tab_p[y] * loc[n, c, y] + tab_rho[y] * later
             loc[n, c, y] = later
+        pltpu.make_async_copy(loc.at[n, c], part_hbm.at[n, c], out_sem.at[i]).start()
         return carry
 
     lax.fori_loop(0, fields, solve, 0)
@@ -467,20 +475,12 @@
     sums = tuple((one * 0.0, one * 0.0) for _ in pairs)
     sums = lax.fori_loop(1, W, gather, sums)
     for (n, c), (f_in, b_in) in zip(pairs, sums):
-        bcar[n, c] = b_in + tail * (fcar[n, c] + phi * f_in)
-        fcar[n, c] = f_in
-
-    def finish(i, carry):
-        n = lax.div(i, ncomp)
-        c = lax.rem(i, ncomp)
-        f_in = fcar[n, c]
-        b_in = bcar[n, c]
-        for y in range(rows):
-            adv_v[n, c, y] = loc[n, c, y] + tab_a[y] * f_in + tab_c[y] * b_in
-        pltpu.make_async_copy(adv_v.at[n, c], adv_hbm.at[n, c], out_sem.at[i]).start()
-        return carry
-
-    lax.fori_loop(0, fields, finish, 0)
+        edges[0, n, c] = f_in
+        edges[1, n, c] = b_in + tail * (fcar[n, c] + phi * f_in)
+    f_out = pltpu.make_async_copy(edges.at[0], f_hbm, out_sem.at[fields + 1])
+    f_out.start()
+    b_out = pltpu.make_async_copy(edges.at[1], b_hbm, out_sem.at[fields + 2])
+    b_out.start()
 
     @pl.when(w < W - 1)
     def _():
@@ -509,11 +509,51 @@
     def drain_out(i, carry):
         n = lax.div(i, ncomp)
         c = lax.rem(i, ncomp)
-        pltpu.make_async_copy(adv_v.at[n, c], adv_hbm.at[n, c], out_sem.at[i]).wait()
+        pltpu.make_async_copy(loc.at[n, c], part_hbm.at[n, c], out_sem.at[i]).wait()
         return carry
 
     lax.fori_loop(0, fields, drain_out, 0)
     advec_out.wait()
+    f_out.wait()
+    b_out.wait()
+    a_out.wait()
+    c_out.wait()
+
+
+def combine(
+    part, explicit, f_in, b_in, a_tab, c_tab, advanced, advection, x, e, f, b, a, c, in_sem, out_sem
+):
+    nvec, ncomp, rows = x.shape[:3]
+    pairs = [(n, m) for n in range(nvec) for m in range(ncomp)]
+    smalls = [
+        pltpu.make_async_copy(src, dst, in_sem.at[k])
+        for k, (src, dst) in enumerate(((f_in, f), (b_in, b), (a_tab, a), (c_tab, c)))
+    ]
+    loads = [
+        pltpu.make_async_copy(part.at[n, m], x.at[n, m], in_sem.at[5 + k])
+        for k, (n, m) in enumerate(pairs)
+    ]
+    stores = [
+        pltpu.make_async_copy(x.at[n, m], advanced.at[n, m], out_sem.at[k])
+        for k, (n, m) in enumerate(pairs)
+    ]
+    e_load = pltpu.make_async_copy(explicit, e, in_sem.at[4])
+    e_store = pltpu.make_async_copy(e, advection, out_sem.at[len(pairs)])
+    for copy in smalls + loads[:1] + [e_load] + loads[1:]:
+        copy.start()
+    for copy in smalls:
+        copy.wait()
+    for k, (n, m) in enumerate(pairs):
+        loads[k].wait()
+        for y in range(rows):
+            x[n, m, y] = x[n, m, y] + a[y] * f[n, m] + c[y] * b[n, m]
+        stores[k].start()
+        if k == 1:
+            e_load.wait()
+            e_store.start()
+    for copy in stores:
+        copy.wait()
+    e_store.wait()
 
 
 def on_device(W, V, q, prev, bs, step, slots, shift, gap, piv, up):
@@ -522,15 +562,21 @@
     field = (nvec, ncomp, rows, nx, nz)
     slab = (ncomp, rows, nx, nz)
     edge = (nvec, ncomp, nx, nz)
-    any_spec = pl.BlockSpec(memory_space=pl.ANY)
     hbm = pl.BlockSpec(memory_space=pltpu.HBM)
     f32, bf16 = jnp.float32, jnp.bfloat16
     dma = pltpu.SemaphoreType.DMA
-    return pl.pallas_call(
+    part, explicit, f_in, b_in, a_tab, c_tab = pl.pallas_call(
         functools.partial(kernel, W, V),
-        out_shape=(jax.ShapeDtypeStruct(field, f32), jax.ShapeDtypeStruct(field, bf16)),
+        out_shape=(
+            jax.ShapeDtypeStruct(field, f32),
+            jax.ShapeDtypeStruct(field, bf16),
+            jax.ShapeDtypeStruct(edge, f32),
+            jax.ShapeDtypeStruct(edge, f32),
+            jax.ShapeDtypeStruct((rows, nx, nz), f32),
+            jax.ShapeDtypeStruct((rows, nx, nz), f32),
+        ),
         in_specs=[hbm] * 9,
-        out_specs=(any_spec, any_spec),
+        out_specs=(hbm,) * 6,
         scratch_shapes=[
             pltpu.SMEM(step.shape, step.dtype),
             pltpu.SMEM(slots.shape, slots.dtype),
@@ -553,7 +599,7 @@
             pltpu.VMEM(slab, bf16),
             pltpu.VMEM(field, f32),
             pltpu.VMEM(field, bf16),
-            pltpu.VMEM(field, f32),
+            pltpu.VMEM((2,) + edge, f32),
             pltpu.VMEM(edge, f32),
             pltpu.VMEM(edge, f32),
             pltpu.VMEM(edge, bf16),
@@ -562,8 +608,9 @@
             pltpu.VMEM((3, nx, 128), f32),
             pltpu.VMEM((W, 3, nx, 128), f32),
         ]
-        + [pltpu.VMEM((rows, nx, nz), f32)] * 6
+        + [pltpu.VMEM((rows, nx, nz), f32)] * 4
         + [
+            pltpu.VMEM((2, rows, nx, nz), f32),
             dma((3,)),
             dma((6,)),
             dma((2,)),
@@ -576,12 +623,29 @@
             dma((chunks,)),
             dma((W,)),
             dma((W,)),
-            dma((nvec * ncomp + 1,)),
+            dma((nvec * ncomp + 5,)),
         ],
         compiler_params=pltpu.CompilerParams(
             collective_id=0, has_side_effects=True, vmem_limit_bytes=63 * 1024 * 1024
         ),
     )(q, prev, bs, step, slots, shift, gap, piv, up)
+    return pl.pallas_call(
+        combine,
+        out_shape=(jax.ShapeDtypeStruct(field, f32), jax.ShapeDtypeStruct(field, bf16)),
+        in_specs=[hbm] * 6,
+        out_specs=(hbm, hbm),
+        scratch_shapes=[
+            pltpu.VMEM(field, f32),
+            pltpu.VMEM(field, bf16),
+            pltpu.VMEM(edge, f32),
+            pltpu.VMEM(edge, f32),
+            pltpu.VMEM((rows, nx, nz), f32),
+            pltpu.VMEM((rows, nx, nz), f32),
+            dma((nvec * ncomp + 5,)),
+            dma((nvec * ncomp + 1,)),
+        ],
+        compiler_params=pltpu.CompilerParams(vmem_limit_bytes=63 * 1024 * 1024),
+    )(part, explicit, f_in, b_in, a_tab, c_tab)
 
 
 def solution(mesh):

time: 28.8 us -> 28.2 us (0.979)
  local copies, waits for them, and re-layouts: 2.95 us -> 0 us
  Pallas kernels: 23.8 us -> 26 us
    unnamed x4 -> x0, local copies, waits for them, and re-layouts: 2.95 us -> none
    pallas_call x0 -> x1, Pallas kernels: none -> 2.52 us  [on_device(): pl.pallas_call(combine, out_shape=(jax.ShapeDtypeStruct(field, f32), jax....]
where the time goes in v4:
time: 28.2 us; the launch traced here: 28 us
  Pallas kernels  26 us (92%)
  between operations  1.93 us (7%)
    pallas_call x1, Pallas kernels, on_device(): pl.pallas_call(functools.partial(kernel, W, V), out_shape=(jax.ShapeDtype...  23.5 us
    pallas_call x1, Pallas kernels, on_device(): pl.pallas_call(combine, out_shape=(jax.ShapeDtypeStruct(field, f32), jax....  2.52 us

profile of v4, /device:TPU:0, one launch (start us, length us, event | category | flops | bytes accessed | tf_op | source)
XLA Modules:
  0.0 28.0 jit_solution(14742292430729659795)
XLA Ops:
  1.9 23.5 %shard_map.104 = (f32[2,3,12,8,384]{4,3,2,1,0:T(8,128)}, bf16[2,3,12,8,384]{4,3,2,1,0:T(8,128)(2,1)}, f32[2,3,8,384]{3,2,1,0:T(8,128)}, f32[2,3,8,384]{3,2,1,0:T...) custom-call(f32[2,3,12,8,384]{4,3,2,1,0:T(8,128)} %q_hbm.1, bf16[2,3,12,8,384]{4,3,2,1,0:T(8,128)(2,1)} %prev_hbm.1, ...), custom_call_target="tpu_custom_call" | custom-call | tf_op jit(solution)/shard_map/pallas_call | solution.py:568
  25.5 2.5 %shard_map.105 = (f32[2,3,12,8,384]{4,3,2,1,0:T(8,128)}, bf16[2,3,12,8,384]{4,3,2,1,0:T(8,128)(2,1)}) custom-call(f32[2,3,12,8,384]{4,3,2,1,0:T(8,128)} %get-tuple-element.8.part, bf16[2,3,12,8,384]{4,3,2,1,0:T(8,128)(2,1)} %get-tuple-element.9.explicit, f32[2,3,8,384]{3,2,1,0:T(8,128)} %get-tuple-element.10.f_in, f32[2,3,8,384]{3,2,1,0:T(8,128)} %get-tuple-element.11.b_in, ...), custom_call_target="tpu_custom_call" | custom-call | tf_op jit(solution)/shard_map/pallas_call | solution.py:632
